TPU v7x, 32 devices: a whole 2x2x4 slice. The times are simulated.
32 devices in a mesh: groups: 2 (over y), resp: 4 (over z), section: 4 (over x, core).
Axes of the slice: x: 2, y: 2, z: 4, core: 2. Of those that a mesh axis runs over, the one named last changes fastest.
Arguments:
- completion_rows: bfloat16 [2, 8, 64, 4096], P(None, ('groups', 'resp')), parts along dimension 1, may hold values from -16 to 16
- prompt_pool: bfloat16 [4, 8, 64, 4096], P('section', ('groups', 'resp')), parts along dimension 1, may hold values from -16 to 16
- norm_gain: float32 [4, 4096], P('section'), may hold values from 0.5 to 1.5
- short_taps: float32 [4, 7, 4096], P('section'), may hold values from -2.4 to 2.4
- long_taps: float32 [4, 128, 256], P('section'), may hold values from -0.5 to 0.5
- score_head: float32 [4096], replicated, may hold values from -0.09375 to 0.09375
- live_lengths: int32 [2, 8], P(None, ('groups', 'resp')), parts along dimension 1, may hold values from 16 to 64, as said below
- prompt_owner: int32 [4], P('groups'), parts along dimension 0, may hold values from 0 to 3
- pair_index: int32 [2, 16, 2], P(None, 'groups'), parts along dimension 1, may hold values from 0 to 3
Outputs:
- scores: bfloat16 [2, 8], P(None, ('groups', 'resp')), parts along dimension 1
- gain_grad: float32 [4, 8192], P('section', 'groups'), parts along dimension 1
- short_grad: float32 [4, 14, 4096], P('section', 'groups'), parts along dimension 1
- long_grad: float32 [4, 256, 256], P('section', 'groups'), parts along dimension 1
There are 2 independent parts, one for each index of `groups`. A program takes and returns all parts, laid end to end along the dimension named above; an argument that names none is the same for every part. Nothing has to cross between parts.
Inputs may be any that keep to these rules, and one draw needn't show every extreme that they name: `live_lengths`: live rows of each completion, counted from its first row; in each microbatch one completion has all 64 rows live and another a quarter of 64. `pair_index`: the two members of a pair may coincide.
All inputs are finite; a program needn't handle non-finite values.
Results may differ from a plain program's by a relative error of at most 0.0097.
Values may be sent and summed in bfloat16 or wider, within the bound.
A program may use at most 256 MiB of HBM per device.

v0:
```python
import jax
import jax.numpy as jnp
from jax import lax
from jax.sharding import PartitionSpec as P


def spread(value, axis, root):
    mine = lax.axis_index(axis) == root
    return lax.psum(jnp.where(mine, value, jnp.zeros_like(value)), axis)


def from_behind(block, axis, distance):
    devices = range(lax.axis_size(axis))
    route = [(i - distance, i) for i in devices if i - distance in devices]
    return lax.ppermute(block, axis, route)


def lag_table(out_rows, all_rows, offset_rows, tap_total):
    lags = (
        offset_rows
        + jnp.arange(out_rows, dtype=jnp.int32)[:, None]
        - jnp.arange(all_rows, dtype=jnp.int32)[None, :]
    )
    return (lags[:, :, None] == jnp.arange(tap_total, dtype=jnp.int32)[None, None, :]).astype(
        jnp.float32
    )


def build_toeplitz(long_row, onehot):
    return jnp.einsum("tsj,jg->gts", onehot, long_row, precision=lax.Precision.HIGHEST)


def fold_toeplitz(toep_grad, onehot):
    return jnp.einsum("tsj,gts->jg", onehot, toep_grad, precision=lax.Precision.HIGHEST)


def filters_apply(joined, normed, short_row, toep, offset_rows):
    count_rows = joined.shape[0]
    channels = joined.shape[1]
    groups_here = toep.shape[0]
    tap_count = short_row.shape[0]
    padded = jnp.pad(normed, ((tap_count - 1, 0), (0, 0)))
    shorter = jnp.zeros_like(normed)
    for offset in range(tap_count):
        begin = tap_count - 1 - offset
        shorter = shorter + short_row[offset][None, :] * padded[begin : begin + count_rows]
    grouped = shorter.reshape(count_rows, groups_here, channels // groups_here)
    longer = jnp.einsum("gts,sgk->tgk", toep, grouped, precision=lax.Precision.HIGHEST)
    longer = longer.reshape(toep.shape[1], channels)
    return joined[offset_rows:] + normed[offset_rows:] * longer


def mixer(comp_rows, prompt_rows, gain_row, short_row, toep):
    joined = jnp.concatenate([prompt_rows, comp_rows], axis=0).astype(jnp.float32)
    factor = lax.rsqrt(jnp.mean(joined * joined, axis=1, keepdims=True) + 1e-06)
    normed = joined * factor * gain_row[None, :]
    return filters_apply(joined, normed, short_row, toep, prompt_rows.shape[0])


def pair_slopes(table, pair_index):
    labels = jnp.arange(table.shape[1], dtype=jnp.int32)
    winner = (pair_index[:, :, 0:1] == labels).astype(jnp.float32)
    loser = (pair_index[:, :, 1:2] == labels).astype(jnp.float32)
    margin = jnp.sum((winner - loser) * table[:, None, :], axis=2)
    weight = jax.nn.sigmoid(-margin)
    return jnp.sum((loser - winner) * weight[:, :, None], axis=1)


def cotangent_rows(slope_arg, head_arg, length_arg, count_rows):
    live = (jnp.arange(count_rows, dtype=jnp.int32) < length_arg).astype(jnp.float32)
    return slope_arg * live[:, None] * head_arg[None, :] / jnp.sqrt(length_arg.astype(jnp.float32))


def score_rows(section_out, head_arg, length_arg):
    per_row = jnp.dot(section_out.astype(jnp.float32), head_arg, precision=lax.Precision.HIGHEST)
    live = jnp.arange(section_out.shape[0], dtype=jnp.int32) < length_arg
    return jnp.sum(jnp.where(live, per_row, 0.0)) / jnp.sqrt(length_arg.astype(jnp.float32))


def put_slot(stored, fresh, chosen, active):
    former = lax.dynamic_index_in_dim(stored, chosen, 0, keepdims=False)
    return lax.dynamic_update_index_in_dim(stored, jnp.where(active, fresh, former), chosen, 0)


def sectioned_run(
    completion_rows,
    prompt_pool,
    norm_gain,
    short_taps,
    long_taps,
    score_head,
    live_lengths,
    prompt_owner,
    pair_index,
):
    sections = lax.axis_size("section")
    section_id = lax.axis_index("section")
    micro_count = completion_rows.shape[0]
    comp_len = completion_rows.shape[2]
    feat_width = completion_rows.shape[3]
    tick_count = sections + micro_count - 1
    gain_row = norm_gain[0]
    short_row = short_taps[0]
    long_row = long_taps[0]
    own_rows = completion_rows[:, 0]
    own_lengths = live_lengths[:, 0]
    local_prompt = prompt_pool[0, 0]
    prompt_len = local_prompt.shape[0]
    is_last = section_id == sections - 1
    is_first = section_id == 0
    batch_labels = jnp.arange(micro_count, dtype=jnp.int32)
    onehot = lag_table(comp_len, prompt_len + comp_len, prompt_len, long_row.shape[0])
    toep = build_toeplitz(long_row, onehot)
    prompt_store = jnp.zeros((micro_count,) + local_prompt.shape, local_prompt.dtype)
    saved_rows = jnp.zeros_like(own_rows)
    own_scores = jnp.zeros((micro_count,), jnp.float32)
    received = jnp.zeros((comp_len, feat_width), jnp.bfloat16)
    for moment in range(tick_count):
        slot_raw = moment - section_id
        active = (slot_raw >= 0) & (slot_raw < micro_count)
        chosen = jnp.clip(slot_raw, 0, micro_count - 1)
        fresh = lax.dynamic_index_in_dim(own_rows, chosen, 0, keepdims=False)
        current = jnp.where(is_first, fresh, received)
        saved_rows = put_slot(saved_rows, current, chosen, active)
        prompt_now = spread(local_prompt, "resp", prompt_owner[chosen])
        prompt_store = put_slot(prompt_store, prompt_now, chosen, active)

        def run_layer():
            return mixer(current, prompt_now, gain_row, short_row, toep).astype(jnp.bfloat16)

        def skip_layer():
            return jnp.zeros((comp_len, feat_width), jnp.bfloat16)

        output = lax.cond(active, run_layer, skip_layer)
        score_now = score_rows(output, score_head, own_lengths[chosen])
        own_scores = jnp.where(active & is_last & (batch_labels == chosen), score_now, own_scores)
        if moment + 1 < tick_count:
            received = from_behind(output, "section", 1)
    table = lax.all_gather(own_scores[:, None], "resp", axis=1, tiled=True)
    slopes = pair_slopes(table, pair_index)
    own_slope = lax.dynamic_slice_in_dim(slopes, lax.axis_index("resp"), 1, 1)[:, 0]
    rounded_scores = own_scores.astype(jnp.bfloat16)
    grad_gain = jnp.zeros_like(gain_row)
    grad_short = jnp.zeros_like(short_row)
    toep_acc = jnp.zeros_like(toep)
    received_grad = jnp.zeros((comp_len, feat_width), jnp.bfloat16)
    known = rounded_scores
    for moment in range(tick_count):
        slot_raw = moment - (sections - 1 - section_id)
        active = (slot_raw >= 0) & (slot_raw < micro_count)
        chosen = jnp.clip(slot_raw, 0, micro_count - 1)
        rows_now = lax.dynamic_index_in_dim(saved_rows, chosen, 0, keepdims=False)
        prompt_now = lax.dynamic_index_in_dim(prompt_store, chosen, 0, keepdims=False)
        head_grad = cotangent_rows(own_slope[chosen], score_head, own_lengths[chosen], comp_len)
        upstream = jnp.where(is_last, head_grad, received_grad.astype(jnp.float32))

        def pull_back():

            def local_layer(rows_var, gain_var, short_var, toep_var):
                return mixer(rows_var, prompt_now, gain_var, short_var, toep_var)

            primal, puller = jax.vjp(local_layer, rows_now, gain_row, short_row, toep)
            return puller(upstream)

        def nothing_back():
            return (
                jnp.zeros((comp_len, feat_width), jnp.bfloat16),
                jnp.zeros_like(gain_row),
                jnp.zeros_like(short_row),
                jnp.zeros_like(toep),
            )

        grad_rows, step_gain, step_short, step_toep = lax.cond(active, pull_back, nothing_back)
        toep_acc = toep_acc + step_toep
        grad_gain = grad_gain + step_gain
        grad_short = grad_short + step_short
        if moment + 1 < tick_count:
            received_grad, passed_scores = from_behind((grad_rows, known), "section", -1)
            known = jnp.where(is_last, rounded_scores, passed_scores)
    grad_long = fold_toeplitz(toep_acc, onehot)
    grad_gain, grad_short, grad_long = lax.psum((grad_gain, grad_short, grad_long), "resp")
    return (known[:, None], grad_gain[None], grad_short[None], grad_long[None])


def body(
    completion_rows,
    prompt_pool,
    norm_gain,
    short_taps,
    long_taps,
    score_head,
    live_lengths,
    prompt_owner,
    pair_index,
):
    results = sectioned_run(
        completion_rows,
        prompt_pool,
        norm_gain,
        short_taps,
        long_taps,
        score_head,
        live_lengths,
        prompt_owner,
        pair_index,
    )
    return results


def solution(mesh):
    placed = (
        P(None, ("groups", "resp"), None, None),
        P("section", ("groups", "resp"), None, None),
        P("section", None),
        P("section", None, None),
        P("section", None, None),
        P(),
        P(None, ("groups", "resp")),
        P("groups"),
        P(None, "groups", None),
    )
    return jax.shard_map(
        body,
        mesh=mesh,
        in_specs=placed,
        out_specs=(
            P(None, ("groups", "resp")),
            P("section", "groups"),
            P("section", "groups", None),
            P("section", "groups", None),
        ),
        check_vma=False,
    )
```

profile of v0, /device:TPU:0, one launch (start us, length us, event | category | flops | bytes accessed | tf_op | source)
XLA Modules:
  0.0 1085.9 jit_solution(16352563520942501082)
XLA Ops:
  29.0 94.0 %all-reduce.96.cloned.1.call-done = (bf16[64,4096]{1,0:T(8,128)(2,1)}, bf16[64,4096]{1,0:T(8,128)(2,1)}, bf16[64,4096]{1,0:T(8,128)(2,1)}, bf16[64,4096]{1,0:T(8,128)(2,1)}, bf16[64,4096]{1,0:T(8,128)(2,1)}) async-done(((bf16[64,4096]{1,0:T(8,128)(2,1)}, bf16[64,4096]{1,0:T(8,128)(2,1)}, bf16[64,4096]{1,0:T(8,128)(2,1)}, bf16[64,4096]{1,0:T(8,128)(2,1)}, bf16[64,4096]{1,0:T(8,128)(2,1)}), ...) | async-done | bytes 2621456 | tf_op jit(solution)/shard_map/psum | solution.py:9
  124.9 43.3 %conditional.10 = (bf16[64,4096]{0,1:T(8,128)(2,1)}) conditional(s32[]{:T(128)} %convert_element_type.230, () %tuple.107, (pred[]{:T(512)}, bf16[1,1,64,4096]{3,2,1,0:T(8,128)(2,1)S(1)}, bf16[64,4096]{1,0:T(8,128)(2,1)S(1)}, bf16[64,4096]{1,0:T(8,128)(2,1)}, f32[1,4096]{1,0:T(1,128)S(1)}, /*index=5*/f32[7,4096]{1,0:T(8,128)S(1)}, ...), branch_computations={%region_5.6_spmd, %region_6.8_spmd} | conditional | flops 418906240 | bytes 61179996 | solution.py:134
  141.5 8.7 copy.120
  150.2 15.8 %fusion.174 = f32[256,16,64]{2,1,0:T(8,128)S(1)} fusion(f32[128,256,16]{0,2,1:T(8,128)} %bitcast.617, f32[256,64,128]{2,1,0:T(8,128)} %copy.120), kind=kOutput, calls=%fused_computation.529 | convolution fusion | flops 402653184 | bytes 11534336 | tf_op jit(solution)/shard_map/cond/branch_1_fun/gts,sgk->tgk/dot_general | solution.py:48
  170.6 13.7 %collective-permute-start = (bf16[64,4096]{1,0:T(8,128)(2,1)}, bf16[64,4096]{1,0:T(8,128)(2,1)}, u32[]{:S(2)}, u32[]{:S(2)}) collective-permute-start(bf16[64,4096]{1,0:T(8,128)(2,1)} %copy.121), channel_id=1, source_target_pairs={{0,1},{1,2},{2,3},{4,5},{5,6},{6,7},{8,9},{9,10},{10,11},{12,13},{... | collective-permute-start | bytes 1572872 | tf_op jit(solution)/shard_map/ppermute | solution.py:15
  214.8 43.1 %conditional.11 = (bf16[64,4096]{0,1:T(8,128)(2,1)S(1)}) conditional(s32[]{:T(128)} %convert_element_type.229, () %tuple.106, (bf16[64,4096]{1,0:T(8,128)(2,1)}, bf16[64,4096]{1,0:T(8,128)(2,1)}, f32[1,4096]{1,0:T(1,128)S(1)}, f32[7,4096]{1,0:T(8,128)S(1)}, f32[256,64,128]{0,2,1:T(8,128)}) %tuple.377), branch_computations={%region_8.9_spmd, %region_9.11_spmd} | conditional | flops 418644096 | bytes 73238648 | solution.py:134
  232.1 8.7 copy.124
  240.9 15.8 %fusion.175 = f32[256,16,64]{2,1,0:T(8,128)S(1)} fusion(f32[128,256,16]{0,2,1:T(8,128)} %bitcast.618, f32[256,64,128]{2,1,0:T(8,128)} %copy.124), kind=kOutput, calls=%fused_computation.530 | convolution fusion | flops 402653184 | bytes 11534336 | tf_op jit(solution)/shard_map/cond/branch_1_fun/gts,sgk->tgk/dot_general | solution.py:48
  274.7 40.2 %collective-permute-start.2 = (bf16[64,4096]{1,0:T(8,128)(2,1)}, bf16[64,4096]{1,0:T(8,128)(2,1)}, u32[]{:S(2)}, u32[]{:S(2)}) collective-permute-start(bf16[64,4096]{1,0:T(8,128)(2,1)} %copy.129), channel_id=1, source_target_pairs={{0,1},{1,2},{2,3},{4,5},{5,6},{6,7},{8,9},{9,10},{10,11},{12,13},{... | collective-permute-start | bytes 1572872 | tf_op jit(solution)/shard_map/ppermute | solution.py:15
  360.8 15.7 %conditional.15 = (bf16[64,4096]{0,1:T(8,128)(2,1)}, f32[4096]{0:T(1024)S(1)}, f32[7,4096]{1,0:T(8,128)S(1)}, f32[256,64,128]{2,1,0:T(8,128)}) conditional(s32[]{:T(128)} %convert_element_type.237, () %tuple.113, (s32[]{:T(128)}, s32[2,1]{0,1:T(1,128)S(1)}, s32[64,1]{0,1:T(1,128)S(1)}, f32[2,4]{1,0:T(2,128)S(1)}, s32[]{:T(128)}, ...), branch_computations={%region_27.28_spmd, %region_28.39_spmd} | conditional | flops 1245062016 | bytes 171630560 | solution.py:173
  380.7 44.2 %collective-permute-done.8 = bf16[64,4096]{1,0:T(8,128)(2,1)} collective-permute-done((bf16[64,4096]{1,0:T(8,128)(2,1)S(1)}, bf16[64,4096]{1,0:T(8,128)(2,1)}, u32[]{:S(2)}, u32[]{:S(2)}) %collective-permute-start.8) | collective-permute-done | bytes 524320 | tf_op jit(solution)/shard_map/ppermute | solution.py:15
  427.0 15.6 %conditional.16 = (bf16[64,4096]{0,1:T(8,128)(2,1)}, f32[4096]{0:T(1024)S(1)}, f32[7,4096]{1,0:T(8,128)S(1)}, f32[256,64,128]{2,1,0:T(8,128)}) conditional(s32[]{:T(128)} %convert_element_type.240, () %tuple.115, (s32[]{:T(128)}, s32[2,1]{0,1:T(1,128)S(1)}, s32[64,1]{0,1:T(1,128)S(1)}, f32[2,4]{1,0:T(2,128)S(1)}, s32[]{:T(128)}, ...), branch_computations={%region_39.40_spmd, %region_40.51_spmd} | conditional | flops 1245062016 | bytes 174776288 | solution.py:173
  446.7 11.4 %collective-permute-done.9 = bf16[64,4096]{1,0:T(8,128)(2,1)} collective-permute-done((bf16[64,4096]{1,0:T(8,128)(2,1)S(1)}, bf16[64,4096]{1,0:T(8,128)(2,1)}, u32[]{:S(2)}, u32[]{:S(2)}) %collective-permute-start.9) | collective-permute-done | bytes 524320 | tf_op jit(solution)/shard_map/ppermute | solution.py:15
  460.2 15.6 %conditional.17 = (bf16[64,4096]{0,1:T(8,128)(2,1)}, f32[4096]{0:T(1024)S(1)}, f32[7,4096]{1,0:T(8,128)S(1)}, f32[256,64,128]{2,1,0:T(8,128)}) conditional(s32[]{:T(128)} %convert_element_type.242, () %tuple.117, (s32[]{:T(128)}, s32[2,1]{0,1:T(1,128)S(1)}, s32[64,1]{0,1:T(1,128)S(1)}, f32[2,4]{1,0:T(2,128)S(1)}, s32[]{:T(128)}, ...), branch_computations={%region_51.52_spmd, %region_52.0_spmd} | conditional | flops 1245062016 | bytes 174776288 | solution.py:173
  481.3 296.5 %collective-permute-done.10 = bf16[64,4096]{1,0:T(8,128)(2,1)} collective-permute-done((bf16[64,4096]{1,0:T(8,128)(2,1)S(1)}, bf16[64,4096]{1,0:T(8,128)(2,1)}, u32[]{:S(2)}, u32[]{:S(2)}) %collective-permute-start.10) | collective-permute-done | bytes 524320 | tf_op jit(solution)/shard_map/ppermute | solution.py:15
  779.8 101.2 %conditional.18 = (bf16[64,4096]{0,1:T(8,128)(2,1)}, f32[4096]{0:T(1024)S(1)}, f32[7,4096]{1,0:T(8,128)S(1)}, f32[256,64,128]{2,1,0:T(8,128)}) conditional(s32[]{:T(128)} %convert_element_type.244, () %tuple.119, (s32[]{:T(128)}, s32[2,1]{0,1:T(1,128)S(1)}, s32[64,1]{0,1:T(1,128)S(1)}, f32[2,4]{1,0:T(2,128)S(1)}, s32[]{:T(128)}, ...), branch_computations={%region_63.64_spmd, %region_64.0_spmd} | conditional | flops 1245062016 | bytes 174776288 | solution.py:173
  793.0 8.7 copy.165
  801.8 16.7 %fusion.187 = f32[256,16,64]{2,1,0:T(8,128)} fusion(f32[128,256,16]{0,2,1:T(8,128)} %bitcast.583, f32[256,64,128]{2,1,0:T(8,128)} %copy.165), kind=kOutput, calls=%fused_computation.542 | convolution fusion | flops 402653184 | bytes 11534336 | tf_op jit(solution)/shard_map/cond/branch_1_fun/jvp(gts,sgk->tgk)/dot_general | solution.py:48
  833.8 10.7 fusion.111
  844.5 11.8 %fusion.105 = (f32[4096]{0:T(1024)S(1)}, f32[4096]{0:T(1024)S(1)}, f32[4096]{0:T(1024)S(1)}, f32[4096]{0:T(1024)S(1)}, f32[4096]{0:T(1024)S(1)}, /*index=5*/f32[...) fusion(f32[256,16,128]{2,1,0:T(8,128)S(1)} %get-tuple-element.1, ...), kind=kLoop, calls=%fused_computation.333 | loop fusion | flops 9936896 | bytes 19087360 | tf_op jit(solution)/shard_map/cond/branch_1_fun/transpose(jvp())/reduce_sum | solution.py:46
  864.0 16.9 %fusion.188 = f32[256,64,128]{2,1,0:T(8,128)} fusion(f32[256,16,64]{2,1,0:T(8,128)} %bitcast.578, f32[128,256,16]{0,2,1:T(8,128)} %bitcast.584), kind=kOutput, calls=%fused_computation.543 | convolution fusion | flops 402653184 | bytes 11534336 | tf_op jit(solution)/shard_map/cond/branch_1_fun/transpose(jvp(gts,sgk->tgk))/dot_general | solution.py:48
  886.5 9.0 collective-permute-done.5
  907.5 99.8 %conditional.19 = (f32[4096]{0:T(1024)S(1)}, f32[7,4096]{1,0:T(8,128)S(1)}, f32[256,64,128]{2,1,0:T(8,128)}) conditional(s32[]{:T(128)} %convert_element_type.246, () %tuple.121, (s32[]{:T(128)}, bf16[2,64,4096]{1,2,0:T(8,128)(2,1)}, bf16[2,64,4096]{1,2,0:T(8,128)(2,1)}, s32[2,1]{0,1:T(1,128)}, s32[64,1]{0,1:T(1,128)}, ...), branch_computations={%region_75.76_spmd, %region_76.86_spmd} | conditional | flops 1244012800 | bytes 143633472 | solution.py:173
  925.2 8.8 copy.168
  934.0 16.7 %fusion.179 = f32[256,16,64]{2,1,0:T(8,128)} fusion(f32[128,256,16]{0,2,1:T(8,128)} %bitcast.587, f32[256,64,128]{2,1,0:T(8,128)} %copy.168), kind=kOutput, calls=%fused_computation.534 | convolution fusion | flops 402653184 | bytes 11534336 | tf_op jit(solution)/shard_map/cond/branch_1_fun/jvp(gts,sgk->tgk)/dot_general | solution.py:48
  961.0 10.6 fusion.125
  971.7 12.2 %fusion.119 = (f32[4096]{0:T(1024)}, f32[4096]{0:T(1024)}, f32[4096]{0:T(1024)}, f32[4096]{0:T(1024)}, f32[4096]{0:T(1024)}, /*index=5*/f32[4096]{0:T(1024)}, f3...) fusion(f32[256,16,128]{2,1,0:T(8,128)S(1)} %get-tuple-element.1, ...), kind=kLoop, calls=%fused_computation.392 | loop fusion | flops 9936896 | bytes 19087360 | tf_op jit(solution)/shard_map/cond/branch_1_fun/transpose(jvp())/reduce_sum | solution.py:46
  990.4 16.6 %fusion.180 = f32[256,64,128]{2,1,0:T(8,128)} fusion(f32[256,16,64]{2,1,0:T(8,128)} %bitcast.590, f32[128,256,16]{0,2,1:T(8,128)S(1)} %bitcast.588), kind=kOutput, calls=%fused_computation.535 | convolution fusion | flops 402653184 | bytes 11534336 | tf_op jit(solution)/shard_map/cond/branch_1_fun/transpose(jvp(gts,sgk->tgk))/dot_general | solution.py:48
  1009.2 19.7 %add_add_fusion.4 = f32[256,64,128]{2,1,0:T(8,128)} fusion(f32[256,64,128]{2,1,0:T(8,128)} %get-tuple-element.909, f32[256,64,128]{2,1,0:T(8,128)} %get-tuple-element.908, f32[256,64,128]{2,1,0:T(8,128)} %get-tuple-element.907, f32[256,64,128]{2,1,0:T(8,128)} %get-tuple-element.905, f32[256,64,128]{2,1,0:T(8,128)} %get-tuple-element.906), kind=kLoop, calls=%fused_computation.412 | loop fusion | flops 8388608 | bytes 50331648 | tf_op jit(solution)/shard_map/add | solution.py:174
  1029.0 13.8 %fusion.133 = f32[1,128,256]{2,1,0:T(8,128)} fusion(f32[256,64,128]{2,1,0:T(8,128)} %add_add_fusion.4, s32[64,128]{1,0:T(8,128)S(1)} %copy-done.89), kind=kOutput, calls=%fused_computation.418 | convolution fusion | flops 3222274048 | bytes 8552448 | tf_op jit(solution)/shard_map/tsj,gts->jg/dot_general | solution.py:34
  1044.1 17.1 %psum.61 = f32[1,4096]{1,0:T(1,128)} all-reduce(f32[1,4096]{1,0:T(1,128)S(1)} %bitcast.746), channel_id=1, replica_groups=mesh['groups'=2,'resp'=4,'section'=4] {'resp'}, use_global_device_ids=true, to_apply=%region_86.87 | all-reduce | flops 4096 | bytes 32768 | tf_op jit(solution)/shard_map/psum | solution.py:181
  1061.2 14.6 %all-reduce.94.cloned.1.call-done = (f32[1,7,4096]{2,0,1:T(1,128)}, f32[1,128,256]{2,1,0:T(8,128)}) async-done(((f32[1,7,4096]{2,0,1:T(1,128)}, f32[1,128,256]{2,1,0:T(8,128)}), (f32[1,7,4096]{2,0,1:T(1,128)}, f32[1,128,256]{2,1,0:T(8,128)})) %all-reduce.94.cloned.1.call-update) | async-done | bytes 245776 | tf_op jit(solution)/shard_map/psum | solution.py:181
  (350 shorter events, 275.7 us)
Async XLA Ops:
  7.2 16.1 %copy-start = (f32[1,128,256]{2,1,0:T(8,128)S(1)}, f32[1,128,256]{2,1,0:T(8,128)}, u32[]{:S(2)}) copy-start(f32[1,128,256]{2,1,0:T(8,128)} %param.33) | copy-start | bytes 393220
  7.2 115.8 %all-reduce.96.cloned.1.call-start = ((), (), s32[]{:S(2)}) async-start(), calls=%async_computation.1 | async-start | bytes 5242880 | tf_op jit(solution)/shard_map/psum | solution.py:9
  14.6 1061.2 %all-reduce.94.cloned.1.call-start = ((), (), s32[]{:S(2)}) async-start(), calls=%async_computation | async-start | bytes 491520 | tf_op jit(solution)/shard_map/psum | solution.py:181
  23.3 101.7 %copy-start.80 = (f32[1,4096]{1,0:T(1,128)S(1)}, f32[1,4096]{1,0:T(1,128)}, u32[]{:S(2)}) copy-start(f32[1,4096]{1,0:T(1,128)} %param.31) | copy-start | bytes 49156
  150.2 15.8 %copy-start.66 = (f32[128,4096]{0,1:T(8,128)S(1)}, f32[128,4096]{0,1:T(8,128)}, u32[]{:S(2)}) copy-start(f32[128,4096]{0,1:T(8,128)} %maximum_convert_fusion) | copy-start | bytes 6291460 | tf_op jit(solution)/shard_map/cond
  170.6 39.4 %collective-permute-start = (bf16[64,4096]{1,0:T(8,128)(2,1)}, bf16[64,4096]{1,0:T(8,128)(2,1)}, u32[]{:S(2)}, u32[]{:S(2)}) collective-permute-start(bf16[64,4096]{1,0:T(8,128)(2,1)} %copy.121), channel_id=1, source_target_pairs={{0,1},{1,2},{2,3},{4,5},{5,6},{6,7},{8,9},{9,10},{10,11},{12,13},{... | collective-permute-start | bytes 1572872 | tf_op jit(solution)/shard_map/ppermute | solution.py:15
  240.8 15.8 %copy-start.18 = (f32[128,4096]{0,1:T(8,128)S(1)}, f32[128,4096]{0,1:T(8,128)}, u32[]{:S(2)}) copy-start(f32[128,4096]{0,1:T(8,128)} %copy-done.17) | copy-start | bytes 6291460 | tf_op jit(solution)/shard_map/cond
  240.8 15.9 %copy-start.67 = (f32[128,4096]{0,1:T(8,128)S(1)}, f32[128,4096]{0,1:T(8,128)}, u32[]{:S(2)}) copy-start(f32[128,4096]{0,1:T(8,128)} %maximum_convert_fusion.1) | copy-start | bytes 6291460 | tf_op jit(solution)/shard_map/cond
  259.0 9.1 collective-permute-start.1
  274.7 47.3 %collective-permute-start.2 = (bf16[64,4096]{1,0:T(8,128)(2,1)}, bf16[64,4096]{1,0:T(8,128)(2,1)}, u32[]{:S(2)}, u32[]{:S(2)}) collective-permute-start(bf16[64,4096]{1,0:T(8,128)(2,1)} %copy.129), channel_id=1, source_target_pairs={{0,1},{1,2},{2,3},{4,5},{5,6},{6,7},{8,9},{9,10},{10,11},{12,13},{... | collective-permute-start | bytes 1572872 | tf_op jit(solution)/shard_map/ppermute | solution.py:15
  328.4 9.2 collective-permute-start.3
  341.3 15.0 %copy-start.81 = (bf16[1,64,4096]{1,2,0:T(8,128)(2,1)S(1)}, bf16[1,64,4096]{1,2,0:T(8,128)(2,1)}, u32[]{:S(2)}) copy-start(bf16[1,64,4096]{1,2,0:T(8,128)(2,1)} %copy.146) | copy-start | bytes 1572868
  356.3 423.5 %copy-start.118 = (f32[2,4]{1,0:T(2,128)}, f32[2,4]{1,0:T(2,128)S(1)}, u32[]{:S(2)}) copy-start(f32[2,4]{1,0:T(2,128)S(1)} %fusion.156) | copy-start | bytes 100
  360.8 419.0 %copy-start.114 = (f32[64,1]{0,1:T(1,128)}, f32[64,1]{0,1:T(1,128)S(1)}, u32[]{:S(2)}) copy-start(f32[64,1]{0,1:T(1,128)S(1)} %broadcast.837) | copy-start | bytes 772
  379.4 45.5 %collective-permute-start.8 = (bf16[64,4096]{1,0:T(8,128)(2,1)S(1)}, bf16[64,4096]{1,0:T(8,128)(2,1)}, u32[]{:S(2)}, u32[]{:S(2)}) collective-permute-start(bf16[64,4096]{1,0:T(8,128)(2,1)S(1)} %copy.157), channel_id=1, source_target_pairs={{1,0},{2,1},{3,2},{5,4},{6,5},{7,6},{9,8},{10,9},{11,10},{13,12},{... | collective-permute-start | bytes 1572872 | tf_op jit(solution)/shard_map/ppermute | solution.py:15
  445.4 12.7 %collective-permute-start.9 = (bf16[64,4096]{1,0:T(8,128)(2,1)S(1)}, bf16[64,4096]{1,0:T(8,128)(2,1)}, u32[]{:S(2)}, u32[]{:S(2)}) collective-permute-start(bf16[64,4096]{1,0:T(8,128)(2,1)S(1)} %copy.160), channel_id=1, source_target_pairs={{1,0},{2,1},{3,2},{5,4},{6,5},{7,6},{9,8},{10,9},{11,10},{13,12},{... | collective-permute-start | bytes 1572872 | tf_op jit(solution)/shard_map/ppermute | solution.py:15
  478.6 299.1 %collective-permute-start.10 = (bf16[64,4096]{1,0:T(8,128)(2,1)S(1)}, bf16[64,4096]{1,0:T(8,128)(2,1)}, u32[]{:S(2)}, u32[]{:S(2)}) collective-permute-start(bf16[64,4096]{1,0:T(8,128)(2,1)S(1)} %copy.163), channel_id=1, source_target_pairs={{1,0},{2,1},{3,2},{5,4},{6,5},{7,6},{9,8},{10,9},{11,10},{13,12},{... | collective-permute-start | bytes 1572872 | tf_op jit(solution)/shard_map/ppermute | solution.py:15
  480.0 405.2 %collective-permute-start.4 = (bf16[2]{0:T(256)(128)(2,1)S(1)}, bf16[2]{0:T(256)(128)(2,1)S(1)}, u32[]{:S(2)}, u32[]{:S(2)}) collective-permute-start(bf16[2]{0:T(256)(128)(2,1)S(1)} %fusion.160), channel_id=1, source_target_pairs={{1,0},{2,1},{3,2},{5,4},{6,5},{7,6},{9,8},{10,9},{11,10},{13,12},{... | collective-permute-start | bytes 20 | tf_op jit(solution)/shard_map/ppermute | solution.py:15
  844.5 11.8 %copy-start.40 = (bf16[128,4096]{0,1:T(8,128)(2,1)S(1)}, bf16[128,4096]{0,1:T(8,128)(2,1)}, u32[]{:S(2)}) copy-start(bf16[128,4096]{0,1:T(8,128)(2,1)} %copy-done.39) | copy-start | bytes 3145732 | tf_op jit(solution)/shard_map/cond
  883.9 22.1 %collective-permute-start.11 = (bf16[64,4096]{1,0:T(8,128)(2,1)S(1)}, bf16[64,4096]{1,0:T(8,128)(2,1)S(1)}, u32[]{:S(2)}, u32[]{:S(2)}) collective-permute-start(bf16[64,4096]{1,0:T(8,128)(2,1)S(1)} %copy.166), channel_id=1, source_target_pairs={{1,0},{2,1},{3,2},{5,4},{6,5},{7,6},{9,8},{10,9},{11,10},{13,12},{... | collective-permute-start | bytes 1572872 | tf_op jit(solution)/shard_map/ppermute | solution.py:15
  885.2 10.3 collective-permute-start.5
  895.5 8.6 collective-permute-start.6
  904.6 138.2 %collective-permute-start.7 = (bf16[2]{0:T(256)(128)(2,1)}, bf16[2]{0:T(256)(128)(2,1)}, u32[]{:S(2)}, u32[]{:S(2)}) collective-permute-start(bf16[2]{0:T(256)(128)(2,1)} %broadcast_select_fusion.1), channel_id=1, source_target_pairs={{1,0},{2,1},{3,2},{5,4},{6,5},{7,6},{9,8},{10,9},{11,10},{13,12},{... | collective-permute-start | bytes 20 | tf_op jit(solution)/shard_map/ppermute | solution.py:15
  907.5 99.8 %copy-start.84 = (f32[7,4096]{1,0:T(8,128)S(1)}, f32[7,4096]{1,0:T(8,128)}, u32[]{:S(2)}) copy-start(f32[7,4096]{1,0:T(8,128)} %copy-done.83) | copy-start | bytes 344068
  990.3 16.6 %copy-start.111 = (f32[4096]{0:T(1024)S(1)}, f32[4096]{0:T(1024)}, u32[]{:S(2)}) copy-start(f32[4096]{0:T(1024)} %fusion.116) | copy-start | bytes 49156 | tf_op jit(solution)/shard_map/cond
  1009.2 19.7 %copy-start.89 = (s32[64,128]{1,0:T(8,128)S(1)}, s32[64,128]{1,0:T(8,128)}, u32[]{:S(2)}) copy-start(s32[64,128]{1,0:T(8,128)} %copy-done.88) | copy-start | bytes 98308
  1028.9 15.1 %copy-start.104 = (f32[4096]{0:T(1024)S(1)}, f32[4096]{0:T(1024)}, u32[]{:S(2)}) copy-start(f32[4096]{0:T(1024)} %copy-done.103) | copy-start | bytes 49156
  1028.9 15.1 %copy-start.106 = (f32[4096]{0:T(1024)S(1)}, f32[4096]{0:T(1024)}, u32[]{:S(2)}) copy-start(f32[4096]{0:T(1024)} %copy-done.105) | copy-start | bytes 49156
  1028.9 15.1 %copy-start.108 = (f32[4096]{0:T(1024)S(1)}, f32[4096]{0:T(1024)}, u32[]{:S(2)}) copy-start(f32[4096]{0:T(1024)} %copy-done.107) | copy-start | bytes 49156
  1028.9 15.1 %copy-start.110 = (f32[4096]{0:T(1024)S(1)}, f32[4096]{0:T(1024)}, u32[]{:S(2)}) copy-start(f32[4096]{0:T(1024)} %copy-done.109) | copy-start | bytes 49156
  1029.0 15.1 %copy-start.113 = (f32[4096]{0:T(1024)S(1)}, f32[4096]{0:T(1024)}, u32[]{:S(2)}) copy-start(f32[4096]{0:T(1024)} %copy-done.112) | copy-start | bytes 49156
  1029.0 49.9 %copy-start.1 = (f32[1,128,256]{2,1,0:T(8,128)S(1)}, f32[1,128,256]{2,1,0:T(8,128)}, u32[]{:S(2)}) copy-start(f32[1,128,256]{2,1,0:T(8,128)} %param.33) | copy-start | bytes 393220
  (58 other events, 289.9 us)
Sparse Core Ops, SparseCore 0:
  14.7 108.2 all-reduce.95
  1042.9 32.8 all-reduce.93
where the time goes:
time: 1090 us
  waiting for transfers between devices  477 us (44%)
  other arithmetic  157 us (14%)
  matrix products  151 us (14%)
  local copies, waits for them, and re-layouts  148 us (14%)
  starting transfers between devices  68.4 us (6%)
  loops' own time  34.5 us (3%)
  blocking collectives  25.6 us (2%)
  between operations  24.9 us (2%)
    ppermute x12, waiting for transfers between devices, from_behind(): return lax.ppermute(block, axis, route)  368 us
    dot_general x8, matrix products, filters_apply(): jnp.einsum('gts,sgk->tgk', toep, grouped, precision=lax.Precision.HIGHEST)  120 us
    psum x1, waiting for transfers between devices, spread(): return lax.psum(jnp.where(mine, value, jnp.zeros_like(value)), axis)  94 us
    ppermute x12, starting transfers between devices, from_behind(): return lax.ppermute(block, axis, route)  68.4 us
    another operation x32, local copies, waits for them, and re-layouts  67.1 us
    add x4, other arithmetic, filters_apply(): shorter + short_row[offset][None, :] * padded[begin:begin + count_rows]  33.5 us
    another operation x5, loops' own time, sectioned_run(): lax.cond(active, pull_back, nothing_back)  33.2 us
    reduce_sum x2, other arithmetic, filters_apply(): short_row[offset][None, :] * padded[begin:begin + count_rows]  24 us
  transfers between devices with their start and end apart: 14, of which 7 were waited for; matrix products, arithmetic and copies ran while one was open for 27% of the time, Pallas kernels for 0%

commit v1 on v0

--- a/solution.py
+++ b/solution.py
@@ -6,7 +6,7 @@
 
 def spread(value, axis, root):
     mine = lax.axis_index(axis) == root
-    return lax.psum(jnp.where(mine, value, jnp.zeros_like(value)), axis)
+    return jnp.sum(lax.all_gather(jnp.where(mine, value, jnp.zeros_like(value)), axis), axis=0)
 
 
 def from_behind(block, axis, distance):

time: 1090 us -> 1150 us (1.055)
  waiting for transfers between devices: 477 us -> 563 us
  local copies, waits for them, and re-layouts: 148 us -> 114 us
    all_gather x0 -> x5, waiting for transfers between devices: none -> 155 us  [spread(): lax.all_gather(jnp.where(mine, value, jnp.zeros_like(value)), axis)]
    psum x1 -> x0, waiting for transfers between devices: 94 us -> none  [spread(): return lax.psum(jnp.where(mine, value, jnp.zeros_like(value)), axis)]
    ppermute x12, waiting for transfers between devices: 368 us -> 391 us  [from_behind(): return lax.ppermute(block, axis, route)]
    dynamic_slice x16 -> x4, local copies, waits for them, and re-layouts: 20.1 us -> 0.99 us  [put_slot(): former = lax.dynamic_index_in_dim(stored, chosen, 0, keepdims=False)]
    broadcast_in_dim x9 -> x0, other arithmetic: 18.8 us -> none  [put_slot(): lax.dynamic_update_index_in_dim(stored, jnp.where(active, fresh, former),...]
    broadcast_in_dim x9 -> x0, local copies, waits for them, and re-layouts: 15.4 us -> none  [put_slot(): lax.dynamic_update_index_in_dim(stored, jnp.where(active, fresh, former),...]
    reduce_sum x0 -> x5, other arithmetic: none -> 13.6 us  [spread(): jnp.sum(lax.all_gather(jnp.where(mine, value, jnp.zeros_like(value)), axi...]
    dynamic_update_slice x0 -> x10, other arithmetic: none -> 12.5 us  [put_slot(): lax.dynamic_update_index_in_dim(stored, jnp.where(active, fresh, former),...]
  transfers between devices with their start and end apart: 14 -> 18, of which waited for: 7 -> 10; matrix products, arithmetic and copies ran while one was open for 27% -> 29% of each run, Pallas kernels for 0% -> 0%
where the time goes in v1:
time: 1150 us
  waiting for transfers between devices  563 us (49%)
  other arithmetic  164 us (14%)
  matrix products  152 us (13%)
  local copies, waits for them, and re-layouts  114 us (10%)
  starting transfers between devices  72.8 us (6%)
  loops' own time  28.9 us (3%)
  blocking collectives  25.6 us (2%)
  between operations  25 us (2%)
    ppermute x12, waiting for transfers between devices, from_behind(): return lax.ppermute(block, axis, route)  391 us
    all_gather x5, waiting for transfers between devices, spread(): lax.all_gather(jnp.where(mine, value, jnp.zeros_like(value)), axis)  155 us
    dot_general x8, matrix products, filters_apply(): jnp.einsum('gts,sgk->tgk', toep, grouped, precision=lax.Precision.HIGHEST)  121 us
    another operation x34, local copies, waits for them, and re-layouts  77.6 us
    ppermute x12, starting transfers between devices, from_behind(): return lax.ppermute(block, axis, route)  72.6 us
    add x4, other arithmetic, filters_apply(): shorter + short_row[offset][None, :] * padded[begin:begin + count_rows]  33.6 us
    another operation x5, loops' own time, sectioned_run(): lax.cond(active, pull_back, nothing_back)  27.4 us
    reduce_sum x2, other arithmetic, filters_apply(): short_row[offset][None, :] * padded[begin:begin + count_rows]  23.4 us
  transfers between devices with their start and end apart: 18, of which 10 were waited for; matrix products, arithmetic and copies ran while one was open for 29% of the time, Pallas kernels for 0%

profile of v1, /device:TPU:0, one launch (start us, length us, event | category | flops | bytes accessed | tf_op | source)
XLA Modules:
  0.0 1145.5 jit_solution(1085544235015009280)
XLA Ops:
  29.3 33.9 %all-gather.20.cloned.1.call-done = bf16[4,1,64,4096]{3,2,1,0:T(8,128)(2,1)} async-done(((bf16[1,1,64,4096]{3,2,1,0:T(8,128)(2,1)}), bf16[4,1,64,4096]{3,2,1,0:T(8,128)(2,1)}) %all-gather.20.cloned.1.call-update) | async-done | bytes 2097168 | tf_op jit(solution)/shard_map/all_gather | solution.py:9
  66.1 43.5 %conditional.10 = (bf16[64,4096]{0,1:T(8,128)(2,1)}) conditional(s32[]{:T(128)} %convert_element_type.240, () %tuple.107, (pred[]{:T(512)}, bf16[1,1,64,4096]{3,2,1,0:T(8,128)(2,1)S(1)}, bf16[64,4096]{1,0:T(8,128)(2,1)}, f32[1,4096]{1,0:T(1,128)S(1)}, f32[7,4096]{1,0:T(8,128)S(1)}, /*index=5*/f32[256,64,128]{0,2,1:T(8,128)}) %tuple.403), branch_computations={%region_5.6_spmd, %region_6.8_spmd} | conditional | flops 418906240 | bytes 63801492 | solution.py:134
  82.9 8.7 copy.150
  91.6 15.8 %fusion.170 = f32[256,16,64]{2,1,0:T(8,128)S(1)} fusion(f32[128,256,16]{0,2,1:T(8,128)} %bitcast.599, f32[256,64,128]{2,1,0:T(8,128)} %copy.150), kind=kOutput, calls=%fused_computation.515 | convolution fusion | flops 402653184 | bytes 11534336 | tf_op jit(solution)/shard_map/cond/branch_1_fun/gts,sgk->tgk/dot_general | solution.py:48
  120.8 35.0 %all-gather.16.cloned.1.call-done = bf16[4,1,64,4096]{3,2,1,0:T(8,128)(2,1)} async-done(((bf16[1,1,64,4096]{3,2,1,0:T(8,128)(2,1)}), bf16[4,1,64,4096]{3,2,1,0:T(8,128)(2,1)}) %all-gather.16.cloned.1.call-update) | async-done | bytes 2097168 | tf_op jit(solution)/shard_map/all_gather | solution.py:9
  157.9 44.1 %all-gather.14.cloned.1.call-done = bf16[4,1,64,4096]{3,2,1,0:T(8,128)(2,1)} async-done(((bf16[1,1,64,4096]{3,2,1,0:T(8,128)(2,1)}), bf16[4,1,64,4096]{3,2,1,0:T(8,128)(2,1)}) %all-gather.14.cloned.1.call-update) | async-done | bytes 2097168 | tf_op jit(solution)/shard_map/all_gather | solution.py:9
  206.5 41.6 %all-gather.12.cloned.1.call-done = bf16[4,1,64,4096]{3,2,1,0:T(8,128)(2,1)} async-done(((bf16[1,1,64,4096]{3,2,1,0:T(8,128)(2,1)}), bf16[4,1,64,4096]{3,2,1,0:T(8,128)(2,1)}) %all-gather.12.cloned.1.call-update) | async-done | bytes 2097168 | tf_op jit(solution)/shard_map/all_gather | solution.py:9
  254.3 43.0 %conditional.11 = (bf16[64,4096]{0,1:T(8,128)(2,1)S(1)}) conditional(s32[]{:T(128)} %convert_element_type.239, () %tuple.106, (bf16[64,4096]{1,0:T(8,128)(2,1)}, bf16[64,4096]{1,0:T(8,128)(2,1)}, f32[1,4096]{1,0:T(1,128)S(1)}, f32[7,4096]{1,0:T(8,128)S(1)}, f32[256,64,128]{0,2,1:T(8,128)}) %tuple.393), branch_computations={%region_8.9_spmd, %region_9.11_spmd} | conditional | flops 418644096 | bytes 73238648 | solution.py:134
  280.3 15.8 %fusion.171 = f32[256,16,64]{2,1,0:T(8,128)S(1)} fusion(f32[128,256,16]{0,2,1:T(8,128)} %bitcast.600, f32[256,64,128]{2,1,0:T(8,128)} %copy.154), kind=kOutput, calls=%fused_computation.516 | convolution fusion | flops 402653184 | bytes 11534336 | tf_op jit(solution)/shard_map/cond/branch_1_fun/gts,sgk->tgk/dot_general | solution.py:48
  307.4 48.9 %collective-permute-start.2 = (bf16[64,4096]{1,0:T(8,128)(2,1)}, bf16[64,4096]{1,0:T(8,128)(2,1)}, u32[]{:S(2)}, u32[]{:S(2)}) collective-permute-start(bf16[64,4096]{1,0:T(8,128)(2,1)} %copy.159), channel_id=1, source_target_pairs={{0,1},{1,2},{2,3},{4,5},{5,6},{6,7},{8,9},{9,10},{10,11},{12,13},{... | collective-permute-start | bytes 1572872 | tf_op jit(solution)/shard_map/ppermute | solution.py:15
  382.6 8.9 all-gather.5
  393.9 14.3 %conditional.15 = (bf16[64,4096]{0,1:T(8,128)(2,1)}, f32[4096]{0:T(1024)S(1)}, f32[7,4096]{1,0:T(8,128)}, f32[256,64,128]{2,1,0:T(8,128)}) conditional(s32[]{:T(128)} %convert_element_type.247, () %tuple.113, (s32[]{:T(128)}, s32[2,1]{0,1:T(1,128)S(1)}, s32[64,1]{0,1:T(1,128)S(1)}, f32[2,4]{1,0:T(2,128)S(1)}, s32[]{:T(128)}, ...), branch_computations={%region_27.28_spmd, %region_28.39_spmd} | conditional | flops 1245062016 | bytes 176292192 | solution.py:173
  411.9 49.0 %collective-permute-done.8 = bf16[64,4096]{1,0:T(8,128)(2,1)} collective-permute-done((bf16[64,4096]{1,0:T(8,128)(2,1)}, bf16[64,4096]{1,0:T(8,128)(2,1)}, u32[]{:S(2)}, u32[]{:S(2)}) %collective-permute-start.8) | collective-permute-done | bytes 524320 | tf_op jit(solution)/shard_map/ppermute | solution.py:15
  462.9 14.3 %conditional.16 = (bf16[64,4096]{0,1:T(8,128)(2,1)}, f32[4096]{0:T(1024)S(1)}, f32[7,4096]{1,0:T(8,128)}, f32[256,64,128]{2,1,0:T(8,128)}) conditional(s32[]{:T(128)} %convert_element_type.250, () %tuple.115, (s32[]{:T(128)}, s32[2,1]{0,1:T(1,128)S(1)}, s32[64,1]{0,1:T(1,128)S(1)}, f32[2,4]{1,0:T(2,128)S(1)}, s32[]{:T(128)}, ...), branch_computations={%region_39.40_spmd, %region_40.51_spmd} | conditional | flops 1245062016 | bytes 179372352 | solution.py:173
  481.0 12.3 %collective-permute-done.9 = bf16[64,4096]{1,0:T(8,128)(2,1)} collective-permute-done((bf16[64,4096]{1,0:T(8,128)(2,1)}, bf16[64,4096]{1,0:T(8,128)(2,1)}, u32[]{:S(2)}, u32[]{:S(2)}) %collective-permute-start.9) | collective-permute-done | bytes 524320 | tf_op jit(solution)/shard_map/ppermute | solution.py:15
  495.4 14.4 %conditional.17 = (bf16[64,4096]{0,1:T(8,128)(2,1)}, f32[4096]{0:T(1024)S(1)}, f32[7,4096]{1,0:T(8,128)}, f32[256,64,128]{2,1,0:T(8,128)}) conditional(s32[]{:T(128)} %convert_element_type.252, () %tuple.117, (s32[]{:T(128)}, s32[2,1]{0,1:T(1,128)S(1)}, s32[64,1]{0,1:T(1,128)S(1)}, f32[2,4]{1,0:T(2,128)S(1)}, s32[]{:T(128)}, ...), branch_computations={%region_51.52_spmd, %region_52.0_spmd} | conditional | flops 1245062016 | bytes 179437920 | solution.py:173
  515.4 314.0 %collective-permute-done.10 = bf16[64,4096]{1,0:T(8,128)(2,1)} collective-permute-done((bf16[64,4096]{1,0:T(8,128)(2,1)}, bf16[64,4096]{1,0:T(8,128)(2,1)}, u32[]{:S(2)}, u32[]{:S(2)}) %collective-permute-start.10) | collective-permute-done | bytes 524320 | tf_op jit(solution)/shard_map/ppermute | solution.py:15
  831.5 108.2 %conditional.18 = (bf16[64,4096]{0,1:T(8,128)(2,1)}, f32[4096]{0:T(1024)S(1)}, f32[7,4096]{1,0:T(8,128)}, f32[256,64,128]{2,1,0:T(8,128)}) conditional(s32[]{:T(128)} %convert_element_type.254, () %tuple.119, (s32[]{:T(128)}, s32[2,1]{0,1:T(1,128)S(1)}, s32[64,1]{0,1:T(1,128)S(1)}, f32[2,4]{1,0:T(2,128)S(1)}, s32[]{:T(128)}, ...), branch_computations={%region_63.64_spmd, %region_64.0_spmd} | conditional | flops 1245062016 | bytes 179372352 | solution.py:173
  858.0 16.7 %fusion.183 = f32[256,16,64]{2,1,0:T(8,128)} fusion(f32[128,256,16]{0,2,1:T(8,128)} %bitcast.565, f32[256,64,128]{2,1,0:T(8,128)} %copy.185), kind=kOutput, calls=%fused_computation.528 | convolution fusion | flops 402653184 | bytes 11534336 | tf_op jit(solution)/shard_map/cond/branch_1_fun/jvp(gts,sgk->tgk)/dot_general | solution.py:48
  890.8 11.3 fusion.111
  902.2 12.0 %fusion.105 = (f32[4096]{0:T(1024)S(1)}, f32[4096]{0:T(1024)}, f32[4096]{0:T(1024)}, f32[4096]{0:T(1024)}, f32[4096]{0:T(1024)}, /*index=5*/f32[4096]{0:T(1024)}...) fusion(f32[256,16,128]{2,1,0:T(8,128)S(1)} %get-tuple-element.1, ...), kind=kLoop, calls=%fused_computation.333 | loop fusion | flops 9936896 | bytes 19087360 | tf_op jit(solution)/shard_map/cond/branch_1_fun/transpose(jvp())/reduce_sum | solution.py:46
  922.6 16.9 %fusion.184 = f32[256,64,128]{2,1,0:T(8,128)} fusion(f32[256,16,64]{2,1,0:T(8,128)} %bitcast.560, f32[128,256,16]{0,2,1:T(8,128)} %bitcast.566), kind=kOutput, calls=%fused_computation.529 | convolution fusion | flops 402653184 | bytes 11534336 | tf_op jit(solution)/shard_map/cond/branch_1_fun/transpose(jvp(gts,sgk->tgk))/dot_general | solution.py:48
  945.4 9.0 collective-permute-done.5
  965.9 101.2 %conditional.19 = (f32[4096]{0:T(1024)S(1)}, f32[7,4096]{1,0:T(8,128)S(1)}, f32[256,64,128]{2,1,0:T(8,128)}) conditional(s32[]{:T(128)} %convert_element_type.256, () %tuple.121, (s32[]{:T(128)}, bf16[2,64,4096]{2,1,0:T(8,128)(2,1)S(1)}, bf16[2,64,4096]{2,1,0:T(8,128)(2,1)}, s32[2,1]{0,1:T(1,128)}, s32[64,1]{0,1:T(1,128)}, ...), branch_computations={%region_75.76_spmd, %region_76.86_spmd} | conditional | flops 1244012800 | bytes 146779168 | solution.py:173
  994.8 16.7 %fusion.175 = f32[256,16,64]{2,1,0:T(8,128)} fusion(f32[128,256,16]{0,2,1:T(8,128)} %bitcast.569, f32[256,64,128]{2,1,0:T(8,128)} %copy.190), kind=kOutput, calls=%fused_computation.520 | convolution fusion | flops 402653184 | bytes 11534336 | tf_op jit(solution)/shard_map/cond/branch_1_fun/jvp(gts,sgk->tgk)/dot_general | solution.py:48
  1021.8 11.0 fusion.125
  1032.8 11.4 fusion.119
  1049.9 16.8 %fusion.176 = f32[256,64,128]{2,1,0:T(8,128)} fusion(f32[256,16,64]{2,1,0:T(8,128)} %bitcast.572, f32[128,256,16]{0,2,1:T(8,128)S(1)} %bitcast.570), kind=kOutput, calls=%fused_computation.521 | convolution fusion | flops 402653184 | bytes 11534336 | tf_op jit(solution)/shard_map/cond/branch_1_fun/transpose(jvp(gts,sgk->tgk))/dot_general | solution.py:48
  1069.1 19.8 %add_add_fusion.4 = f32[256,64,128]{2,1,0:T(8,128)} fusion(f32[256,64,128]{2,1,0:T(8,128)} %get-tuple-element.908, f32[256,64,128]{2,1,0:T(8,128)} %get-tuple-element.907, f32[256,64,128]{2,1,0:T(8,128)} %get-tuple-element.906, f32[256,64,128]{2,1,0:T(8,128)} %get-tuple-element.904, f32[256,64,128]{2,1,0:T(8,128)} %get-tuple-element.905), kind=kLoop, calls=%fused_computation.412 | loop fusion | flops 8388608 | bytes 50331648 | tf_op jit(solution)/shard_map/add | solution.py:174
  1088.9 13.8 %fusion.133 = f32[1,128,256]{2,1,0:T(8,128)} fusion(f32[256,64,128]{2,1,0:T(8,128)} %add_add_fusion.4, s32[64,128]{1,0:T(8,128)S(1)} %copy-done.90), kind=kOutput, calls=%fused_computation.418 | convolution fusion | flops 3222274048 | bytes 8552448 | tf_op jit(solution)/shard_map/tsj,gts->jg/dot_general | solution.py:34
  1104.0 16.7 %psum.21 = f32[1,4096]{1,0:T(1,128)} all-reduce(f32[1,4096]{1,0:T(1,128)S(1)} %bitcast.728), channel_id=1, replica_groups=mesh['groups'=2,'resp'=4,'section'=4] {'resp'}, use_global_device_ids=true, to_apply=%region_86.87 | all-reduce | flops 4096 | bytes 32768 | tf_op jit(solution)/shard_map/psum | solution.py:181
  1120.8 14.6 %all-reduce.92.cloned.1.call-done = (f32[1,7,4096]{2,0,1:T(1,128)}, f32[1,128,256]{2,1,0:T(8,128)}) async-done(((f32[1,7,4096]{2,0,1:T(1,128)}, f32[1,128,256]{2,1,0:T(8,128)}), (f32[1,7,4096]{2,0,1:T(1,128)}, f32[1,128,256]{2,1,0:T(8,128)})) %all-reduce.92.cloned.1.call-update) | async-done | bytes 245776 | tf_op jit(solution)/shard_map/psum | solution.py:181
  (371 shorter events, 279.0 us)
Async XLA Ops:
  7.2 56.0 %all-gather.20.cloned.1.call-start = ((), (), s32[]{:S(2)}) async-start(), calls=%async_computation.4 | async-start | bytes 2621440 | tf_op jit(solution)/shard_map/all_gather | solution.py:9
  14.5 103.3 %all-gather.18.cloned.1.call-start = ((), (), s32[]{:S(2)}) async-start(), calls=%async_computation.3 | async-start | bytes 2621440 | tf_op jit(solution)/shard_map/all_gather | solution.py:9
  15.3 140.6 %all-gather.16.cloned.1.call-start = ((), (), s32[]{:S(2)}) async-start(), calls=%async_computation.2 | async-start | bytes 2621440 | tf_op jit(solution)/shard_map/all_gather | solution.py:9
  16.0 185.9 %all-gather.14.cloned.1.call-start = ((), (), s32[]{:S(2)}) async-start(), calls=%async_computation.1 | async-start | bytes 2621440 | tf_op jit(solution)/shard_map/all_gather | solution.py:9
  16.6 231.5 %all-gather.12.cloned.1.call-start = ((), (), s32[]{:S(2)}) async-start(), calls=%async_computation | async-start | bytes 2621440 | tf_op jit(solution)/shard_map/all_gather | solution.py:9
  17.2 1118.2 %all-reduce.92.cloned.1.call-start = ((), (), s32[]{:S(2)}) async-start(), calls=%async_computation.5 | async-start | bytes 491520 | tf_op jit(solution)/shard_map/psum | solution.py:181
  66.1 48.1 %copy-start.84 = (f32[4096]{0:T(1024)S(1)}, f32[4096]{0:T(1024)}, u32[]{:S(2)}) copy-start(f32[4096]{0:T(1024)} %param.34) | copy-start | bytes 49156
  111.9 140.2 %collective-permute-start = (bf16[64,4096]{1,0:T(8,128)(2,1)}, bf16[64,4096]{1,0:T(8,128)(2,1)}, u32[]{:S(2)}, u32[]{:S(2)}) collective-permute-start(bf16[64,4096]{1,0:T(8,128)(2,1)} %copy.151), channel_id=1, source_target_pairs={{0,1},{1,2},{2,3},{4,5},{5,6},{6,7},{8,9},{9,10},{10,11},{12,13},{... | collective-permute-start | bytes 1572872 | tf_op jit(solution)/shard_map/ppermute | solution.py:15
  157.8 48.4 %copy-start.82 = (bf16[64,4096]{1,0:T(8,128)(2,1)}, bf16[64,4096]{1,0:T(8,128)(2,1)S(1)}, u32[]{:S(2)}) copy-start(bf16[64,4096]{1,0:T(8,128)(2,1)S(1)} %reduce_sum.883) | copy-start | bytes 1572868
  157.9 47.1 %copy-start.81 = (bf16[64,4096]{1,0:T(8,128)(2,1)S(1)}, bf16[64,4096]{1,0:T(8,128)(2,1)}, u32[]{:S(2)}) copy-start(bf16[64,4096]{1,0:T(8,128)(2,1)} %reduce_sum.885) | copy-start | bytes 1572868
  206.4 45.7 %copy-start.66 = (bf16[2,1,64,4096]{3,2,1,0:T(8,128)(2,1)S(1)}, bf16[2,1,64,4096]{3,2,1,0:T(8,128)(2,1)}, u32[]{:S(2)}) copy-start(bf16[2,1,64,4096]{3,2,1,0:T(8,128)(2,1)} %param.29) | copy-start | bytes 3145732
  298.4 5.2 collective-permute-start.1
  307.4 51.4 %collective-permute-start.2 = (bf16[64,4096]{1,0:T(8,128)(2,1)}, bf16[64,4096]{1,0:T(8,128)(2,1)}, u32[]{:S(2)}, u32[]{:S(2)}) collective-permute-start(bf16[64,4096]{1,0:T(8,128)(2,1)} %copy.159), channel_id=1, source_target_pairs={{0,1},{1,2},{2,3},{4,5},{5,6},{6,7},{8,9},{9,10},{10,11},{12,13},{... | collective-permute-start | bytes 1572872 | tf_op jit(solution)/shard_map/ppermute | solution.py:15
  362.5 10.9 collective-permute-start.3
  408.2 54.8 %copy-start.104 = (f32[4096]{0:T(1024)}, f32[4096]{0:T(1024)S(1)}, u32[]{:S(2)}) copy-start(f32[4096]{0:T(1024)S(1)} %get-tuple-element.890) | copy-start | bytes 49156
  408.2 54.8 %copy-start.138 = (f32[64,1]{0,1:T(1,128)S(1)}, f32[64,1]{0,1:T(1,128)}, u32[]{:S(2)}) copy-start(f32[64,1]{0,1:T(1,128)} %copy-done.137) | copy-start | bytes 772
  408.2 54.7 %copy-start.143 = (s32[2,1]{0,1:T(1,128)S(1)}, s32[2,1]{0,1:T(1,128)}, u32[]{:S(2)}) copy-start(s32[2,1]{0,1:T(1,128)} %param.35) | copy-start | bytes 28
  408.2 54.7 %copy-start.148 = (f32[2,4]{1,0:T(2,128)S(1)}, f32[2,4]{1,0:T(2,128)}, u32[]{:S(2)}) copy-start(f32[2,4]{1,0:T(2,128)} %copy-done.147) | copy-start | bytes 100
  410.6 50.3 %collective-permute-start.8 = (bf16[64,4096]{1,0:T(8,128)(2,1)}, bf16[64,4096]{1,0:T(8,128)(2,1)}, u32[]{:S(2)}, u32[]{:S(2)}) collective-permute-start(bf16[64,4096]{1,0:T(8,128)(2,1)} %copy.171), channel_id=1, source_target_pairs={{1,0},{2,1},{3,2},{5,4},{6,5},{7,6},{9,8},{10,9},{11,10},{13,12},{... | collective-permute-start | bytes 1572872 | tf_op jit(solution)/shard_map/ppermute | solution.py:15
  479.7 13.6 %collective-permute-start.9 = (bf16[64,4096]{1,0:T(8,128)(2,1)}, bf16[64,4096]{1,0:T(8,128)(2,1)}, u32[]{:S(2)}, u32[]{:S(2)}) collective-permute-start(bf16[64,4096]{1,0:T(8,128)(2,1)} %copy.176), channel_id=1, source_target_pairs={{1,0},{2,1},{3,2},{5,4},{6,5},{7,6},{9,8},{10,9},{11,10},{13,12},{... | collective-permute-start | bytes 1572872 | tf_op jit(solution)/shard_map/ppermute | solution.py:15
  509.8 321.6 %copy-start.108 = (f32[4096]{0:T(1024)}, f32[4096]{0:T(1024)S(1)}, u32[]{:S(2)}) copy-start(f32[4096]{0:T(1024)S(1)} %get-tuple-element.894) | copy-start | bytes 49156
  509.8 321.6 %copy-start.140 = (f32[64,1]{0,1:T(1,128)S(1)}, f32[64,1]{0,1:T(1,128)}, u32[]{:S(2)}) copy-start(f32[64,1]{0,1:T(1,128)} %copy-done.137) | copy-start | bytes 772
  509.8 321.6 %copy-start.145 = (s32[2,1]{0,1:T(1,128)S(1)}, s32[2,1]{0,1:T(1,128)}, u32[]{:S(2)}) copy-start(s32[2,1]{0,1:T(1,128)} %param.35) | copy-start | bytes 28
  509.9 321.6 %copy-start.150 = (f32[2,4]{1,0:T(2,128)S(1)}, f32[2,4]{1,0:T(2,128)}, u32[]{:S(2)}) copy-start(f32[2,4]{1,0:T(2,128)} %copy-done.147) | copy-start | bytes 100
  512.2 317.1 %collective-permute-start.10 = (bf16[64,4096]{1,0:T(8,128)(2,1)}, bf16[64,4096]{1,0:T(8,128)(2,1)}, u32[]{:S(2)}, u32[]{:S(2)}) collective-permute-start(bf16[64,4096]{1,0:T(8,128)(2,1)} %copy.181), channel_id=1, source_target_pairs={{1,0},{2,1},{3,2},{5,4},{6,5},{7,6},{9,8},{10,9},{11,10},{13,12},{... | collective-permute-start | bytes 1572872 | tf_op jit(solution)/shard_map/ppermute | solution.py:15
  514.1 429.3 %collective-permute-start.4 = (bf16[2]{0:T(256)(128)(2,1)}, bf16[2]{0:T(256)(128)(2,1)}, u32[]{:S(2)}, u32[]{:S(2)}) collective-permute-start(bf16[2]{0:T(256)(128)(2,1)} %fusion.156), channel_id=1, source_target_pairs={{1,0},{2,1},{3,2},{5,4},{6,5},{7,6},{9,8},{10,9},{11,10},{13,12},{... | collective-permute-start | bytes 20 | tf_op jit(solution)/shard_map/ppermute | solution.py:15
  840.0 50.8 %copy-start.158 = (f32[128]{0:T(128)}, f32[128]{0:T(128)S(1)}, u32[]{:S(2)}) copy-start(f32[128]{0:T(128)S(1)} %fusion.113) | copy-start | bytes 1540 | tf_op jit(solution)/shard_map/cond
  942.1 22.3 %collective-permute-start.11 = (bf16[64,4096]{1,0:T(8,128)(2,1)}, bf16[64,4096]{1,0:T(8,128)(2,1)S(1)}, u32[]{:S(2)}, u32[]{:S(2)}) collective-permute-start(bf16[64,4096]{1,0:T(8,128)(2,1)} %copy.186), channel_id=1, source_target_pairs={{1,0},{2,1},{3,2},{5,4},{6,5},{7,6},{9,8},{10,9},{11,10},{13,12},{... | collective-permute-start | bytes 1572872 | tf_op jit(solution)/shard_map/ppermute | solution.py:15
  944.1 10.3 collective-permute-start.5
  954.4 8.1 collective-permute-start.6
  963.1 139.7 %collective-permute-start.7 = (bf16[2]{0:T(256)(128)(2,1)}, bf16[2]{0:T(256)(128)(2,1)}, u32[]{:S(2)}, u32[]{:S(2)}) collective-permute-start(bf16[2]{0:T(256)(128)(2,1)} %broadcast_select_fusion.6), channel_id=1, source_target_pairs={{1,0},{2,1},{3,2},{5,4},{6,5},{7,6},{9,8},{10,9},{11,10},{13,12},{... | collective-permute-start | bytes 20 | tf_op jit(solution)/shard_map/ppermute | solution.py:15
  1088.9 49.6 %copy-start.1 = (f32[1,128,256]{2,1,0:T(8,128)S(1)}, f32[1,128,256]{2,1,0:T(8,128)}, u32[]{:S(2)}) copy-start(f32[1,128,256]{2,1,0:T(8,128)} %param.33) | copy-start | bytes 393220
  (78 other events, 687.4 us)
Sparse Core Ops, SparseCore 0:
  14.7 48.4 all-gather.19
  64.8 44.8 all-gather.17
  111.2 44.6 all-gather.15
  157.3 44.6 all-gather.13
  203.4 44.6 all-gather.11
  1102.9 32.4 all-reduce.91
